TPU v7x, 32 devices: a whole 2x2x4 slice. The times are simulated.
32 devices in a mesh: parts: 2 (over x), harm: 4 (over y, core), tile: 4 (over z).
Axes of the slice: x: 2, y: 2, z: 4, core: 2. Of those that a mesh axis runs over, the one named last changes fastest.
Arguments:
- perturbation: float32 [8, 2, 5, 128, 256], P('harm', None, None, ('parts', 'tile')), parts along dimension 3, may hold values from -6 to 6
- base_flow: float32 [8, 2, 3, 128, 256], P('harm', None, None, ('parts', 'tile')), parts along dimension 3, may hold values from -0.9 to 0.9
- viscosity: float32 [128, 256], P(('parts', 'tile')), parts along dimension 0, may hold values from 0.05 to 0.5
Outputs:
- resolvent_image: float32 [8, 2, 5, 128, 256], P('harm', None, None, ('parts', 'tile')), parts along dimension 3
There are 2 independent parts, one for each index of `parts`. A program takes and returns all parts, laid end to end along the dimension named above; each array names one. Nothing has to cross between parts.
All inputs are finite; a program needn't handle non-finite values.
Results may differ from a plain program's by a relative error of at most 0.00002.
Values sent between devices are 32-bit elements; how exact they have to be, the bound alone decides.
A program may use at most 64 MiB of HBM per device.

v0:
```python
import jax
import jax.numpy as jnp
import numpy as np
from jax import lax
from jax.sharding import PartitionSpec as P

omega_base = 0.25


def extended(cells, sides, width):
    for axis, dim in sides:
        count = lax.axis_size(axis)
        head = lax.slice_in_dim(cells, 0, width, axis=dim)
        tail = lax.slice_in_dim(cells, cells.shape[dim] - width, cells.shape[dim], axis=dim)
        cells = jnp.concatenate(
            [
                lax.ppermute(tail, axis, [(i, (i + 1) % count) for i in range(count)]),
                cells,
                lax.ppermute(head, axis, [((i + 1) % count, i) for i in range(count)]),
            ],
            axis=dim,
        )
    return cells


def shifted(value, axis, steps):
    count = lax.axis_size(axis)
    pairs = [(source, (source + steps) % count) for source in range(count)]
    return lax.ppermute(value, axis, pairs)


def split_rows(padded):
    middle = padded[..., 1:-1, :]
    grad_x = 0.5 * (padded[..., 2:, :] - padded[..., :-2, :])
    grad_y = 0.5 * (jnp.roll(middle, -1, -1) - jnp.roll(middle, 1, -1))
    return (middle, grad_x, grad_y)


def diffusion(padded, visc_padded):
    middle = padded[..., 1:-1, :]
    center = visc_padded[1:-1]
    east_face = 0.5 * (center + visc_padded[2:])
    west_face = 0.5 * (center + visc_padded[:-2])
    north_face = 0.5 * (center + jnp.roll(center, -1, -1))
    south_face = 0.5 * (center + jnp.roll(center, 1, -1))
    return (
        east_face * (padded[..., 2:, :] - middle)
        - west_face * (middle - padded[..., :-2, :])
        + north_face * (jnp.roll(middle, -1, -1) - middle)
        - south_face * (middle - jnp.roll(middle, 1, -1))
    )


def acoustic(grad_x, grad_y):
    dilation = grad_x[..., 1, :, :] + grad_y[..., 2, :, :]
    return jnp.stack(
        [dilation, grad_x[..., 4, :, :], grad_y[..., 4, :, :], jnp.zeros_like(dilation), dilation],
        axis=-3,
    )


def own_terms(middle, grad_x, grad_y, damping, frequency):
    rotation = jnp.stack([-frequency * middle[:, 1], frequency * middle[:, 0]], axis=1)
    return rotation + acoustic(grad_x, grad_y) - damping


def coupling(
    u_real, u_imag, v_real, v_imag, g_real, g_imag, q_real, q_imag, x_real, x_imag, y_real, y_imag
):
    real_part = (
        u_real * x_real
        - u_imag * x_imag
        + v_real * y_real
        - v_imag * y_imag
        + g_real * q_real
        - g_imag * q_imag
    )
    imag_part = (
        u_real * x_imag
        + u_imag * x_real
        + v_real * y_imag
        + v_imag * y_real
        + g_real * q_imag
        + g_imag * q_real
    )
    return (real_part, imag_part)


def block_terms(blocks, middle, grad_x, grad_y):
    local_count = middle.shape[0]
    index_table = np.array(
        [
            [local_count + target - source for source in range(local_count)]
            for target in range(local_count)
        ],
        dtype=np.int32,
    )
    chosen = blocks[index_table]

    def base_part(complex_index, field_index):
        return chosen[:, :, complex_index, field_index][:, :, None]

    def moved_part(values, complex_index):
        return values[None, :, complex_index]

    real_part, imag_part = coupling(
        base_part(0, 0),
        base_part(1, 0),
        base_part(0, 1),
        base_part(1, 1),
        base_part(0, 2),
        base_part(1, 2),
        moved_part(middle, 0),
        moved_part(middle, 1),
        moved_part(grad_x, 0),
        moved_part(grad_x, 1),
        moved_part(grad_y, 0),
        moved_part(grad_y, 1),
    )
    return jnp.stack([jnp.sum(real_part, axis=1), jnp.sum(imag_part, axis=1)], axis=1)


def shards(perturbation, base_flow, viscosity):
    local_count = perturbation.shape[0]
    width_x = perturbation.shape[3]
    width_y = perturbation.shape[4]
    groups = lax.axis_size("harm")
    first_index = lax.axis_index("harm") * local_count
    flattened = perturbation.reshape(local_count * 10, width_x, width_y)
    stacked = jnp.concatenate([flattened, viscosity[None]], axis=0)
    padded = extended(stacked, (("tile", 1),), 1)
    own_padded = padded[:-1].reshape(local_count, 2, 5, width_x + 2, width_y)
    visc_padded = padded[-1]
    numbers = first_index + jnp.arange(local_count, dtype=jnp.int32)
    total_count = local_count * groups
    signed = jnp.where(numbers < total_count // 2, numbers, numbers - total_count)
    frequency = (omega_base * signed.astype(jnp.float32)).reshape(local_count, 1, 1, 1)
    middle, grad_x, grad_y = split_rows(own_padded)
    summed = own_terms(middle, grad_x, grad_y, diffusion(own_padded, visc_padded), frequency)
    whole_base = lax.all_gather(base_flow, "harm", axis=0, tiled=True)

    def base_pair(position, earlier):
        before = lax.dynamic_slice_in_dim(
            whole_base, (position + groups - 1) % groups * local_count, local_count, 0
        )
        current = lax.dynamic_slice_in_dim(whole_base, position * local_count, local_count, 0)
        return (jnp.concatenate([before, current], axis=0), earlier)

    earlier = base_flow
    moving = own_padded

    def advance(moving):
        moved = shifted(moving, "harm", 1)
        return (moved, moved)

    blocks, earlier = base_pair(0, earlier)
    summed = summed + block_terms(blocks, middle, grad_x, grad_y)

    def advance_step(position, carried):
        summed, moving, earlier = carried
        moving, rimmed = advance(moving)
        blocks, earlier = base_pair(position, earlier)
        values, slope_x, slope_y = split_rows(rimmed)
        return (summed + block_terms(blocks, values, slope_x, slope_y), moving, earlier)

    summed, moving, earlier = lax.fori_loop(1, groups, advance_step, (summed, moving, earlier))
    return summed


def solution(mesh):
    placed = (
        P("harm", None, None, ("parts", "tile"), None),
        P("harm", None, None, ("parts", "tile"), None),
        P(("parts", "tile"), None),
    )
    return jax.shard_map(
        shards,
        mesh=mesh,
        in_specs=placed,
        out_specs=P("harm", None, None, ("parts", "tile"), None),
        check_vma=False,
    )
```

profile of v0, /device:TPU:0, one launch (start us, length us, event | category | flops | bytes accessed | tf_op | source)
XLA Modules:
  0.0 47.7 jit_solution(18082950959541213090)
XLA Ops:
  0.0 1.1 %pad_maximum_fusion.8 = (f32[21,1,256]{2,1,0:T(1,128)S(1)}, f32[21,1,256]{2,1,0:T(1,128)S(1)}) fusion(f32[1,16,256]{2,1,0:T(8,128)} %bitcast.94, f32[20,16,256]{2,1,0:T(8,128)} %bitcast.90), kind=kLoop, calls=%fused_computation.57 | loop fusion | flops 10752 | bytes 387072 | tf_op jit(solution)/shard_map/slice | solution.py:14
  1.1 5.1 %collective-permute-start.2 = (f32[21,1,256]{2,1,0:T(1,128)S(1)}, f32[21,1,256]{2,1,0:T(1,128)S(1)}, u32[]{:S(2)}, u32[]{:S(2)}) collective-permute-start(f32[21,1,256]{2,1,0:T(1,128)S(1)} %get-tuple-element.304), channel_id=1, source_target_pairs={{1,0},{2,1},{3,2},{0,3},{5,4},{6,5},{7,6},{4,7},{9,8},{10,9},{11,1... | collective-permute-start | bytes 64520 | tf_op jit(solution)/shard_map/ppermute | solution.py:19
  6.4 8.6 %all_gather.3 = f32[8,2,3,16,256]{4,3,2,1,0:T(8,128)S(1)} all-gather(f32[2,2,3,16,256]{4,3,2,1,0:T(8,128)S(1)} %copy-done.2), channel_id=1, replica_groups=mesh['parts'=2,'harm'=4,'tile'=4] {'harm'}, dimensions={0}, use_global_device_ids=true | all-gather | bytes 983040 | tf_op jit(solution)/shard_map/all_gather | solution.py:140
  15.0 0.6 %copy-done.3 = s32[4]{0:T(128)S(1)} copy-done((s32[4]{0:T(128)S(1)}, s32[4]{0:T(128)}, u32[]{:S(2)}) %copy-start.3) | copy-done | bytes 40
  15.7 0.6 %gather_fusion.1 = f32[4,2,3,16,256]{4,3,2,1,0:T(8,128)S(1)} fusion(f32[4,2,3,16,256]{4,3,2,1,0:T(8,128)S(1)} %pad_maximum_fusion.4, s32[1024]{0:T(1024)S(1)} %pad_clamp_fusion.1), kind=kCustom, calls=%fused_computation.1 | custom fusion | bytes 786448 | tf_op jit(solution)/shard_map/gather | solution.py:98
  16.4 0.9 %copy-done = f32[2,2,5,16,256]{4,3,2,1,0:T(8,128)S(1)} copy-done((f32[2,2,5,16,256]{4,3,2,1,0:T(8,128)S(1)}, f32[2,2,5,16,256]{4,3,2,1,0:T(8,128)}, u32[]{:S(2)}) %copy-start) | copy-done | bytes 327704
  17.3 0.2 fusion.20
  17.5 0.1 fusion.21
  17.6 0.2 subtract_multiply_fusion
  18.1 0.3 subtract_reduce_fusion.1
  18.5 0.3 fusion.3
  18.8 28.2 %while.21 = (s32[]{:T(128)}, f32[2,2,5,16,256]{4,3,2,0,1:T(8,128)S(1)}, f32[2,2,5,18,256]{4,3,2,0,1:T(8,128)S(1)}, f32[8,2,3,16,256]{4,3,2,1,0:T(8,128)S(1)}, s3...) while((s32[]{:T(128)}, ...), condition=%wide.region_5.6_spmd.clone, body=%wide.region_2.5_spmd.sunk.clone.sunk | while | flops 2638870 | bytes 13291922 | solution.py:166
  18.8 0.4 collective-permute-start
  19.3 0.6 %gather_fusion = f32[4,2,3,16,256]{4,3,2,1,0:T(8,128)S(1)} fusion(f32[4,2,3,16,256]{4,3,2,1,0:T(8,128)S(1)} %pad_maximum_fusion.14, s32[1024]{0:T(1024)S(1)} %pad_clamp_fusion.3), kind=kCustom, calls=%fused_computation.clone.1 | custom fusion | bytes 786448 | tf_op jit(solution)/shard_map/while/body/eval_jaxpr/gather | solution.py:98
  19.9 7.2 %collective-permute-done = f32[2,2,5,18,256]{4,3,2,0,1:T(8,128)S(1)} collective-permute-done((f32[2,2,5,18,256]{4,3,2,0,1:T(8,128)S(1)}, f32[2,2,5,18,256]{4,3,2,0,1:T(8,128)S(1)}, u32[]{:S(2)}, u32[]{:S(2)}) %collective-permute-start) | collective-permute-done | bytes 368672 | tf_op jit(solution)/shard_map/while/body/eval_jaxpr/ppermute | solution.py:29
  27.2 0.1 fusion.33
  27.3 0.2 fusion.34
  27.5 0.2 fusion.35
  27.8 0.3 subtract_reduce_fusion.3
  28.4 0.6 %gather_fusion = f32[4,2,3,16,256]{4,3,2,1,0:T(8,128)S(1)} fusion(f32[4,2,3,16,256]{4,3,2,1,0:T(8,128)S(1)} %pad_maximum_fusion.14, s32[1024]{0:T(1024)S(1)} %pad_clamp_fusion.3), kind=kCustom, calls=%fused_computation.clone.1 | custom fusion | bytes 786448 | tf_op jit(solution)/shard_map/while/body/eval_jaxpr/gather | solution.py:98
  29.0 7.5 %collective-permute-done = f32[2,2,5,18,256]{4,3,2,0,1:T(8,128)S(1)} collective-permute-done((f32[2,2,5,18,256]{4,3,2,0,1:T(8,128)S(1)}, f32[2,2,5,18,256]{4,3,2,0,1:T(8,128)S(1)}, u32[]{:S(2)}, u32[]{:S(2)}) %collective-permute-start) | collective-permute-done | bytes 368672 | tf_op jit(solution)/shard_map/while/body/eval_jaxpr/ppermute | solution.py:29
  36.6 0.1 fusion.33
  36.7 0.2 fusion.34
  36.9 0.2 fusion.35
  37.2 0.3 subtract_reduce_fusion.3
  37.8 0.6 %gather_fusion = f32[4,2,3,16,256]{4,3,2,1,0:T(8,128)S(1)} fusion(f32[4,2,3,16,256]{4,3,2,1,0:T(8,128)S(1)} %pad_maximum_fusion.14, s32[1024]{0:T(1024)S(1)} %pad_clamp_fusion.3), kind=kCustom, calls=%fused_computation.clone.1 | custom fusion | bytes 786448 | tf_op jit(solution)/shard_map/while/body/eval_jaxpr/gather | solution.py:98
  38.4 7.5 %collective-permute-done = f32[2,2,5,18,256]{4,3,2,0,1:T(8,128)S(1)} collective-permute-done((f32[2,2,5,18,256]{4,3,2,0,1:T(8,128)S(1)}, f32[2,2,5,18,256]{4,3,2,0,1:T(8,128)S(1)}, u32[]{:S(2)}, u32[]{:S(2)}) %collective-permute-start) | collective-permute-done | bytes 368672 | tf_op jit(solution)/shard_map/while/body/eval_jaxpr/ppermute | solution.py:29
  46.0 0.1 fusion.33
  46.1 0.2 fusion.34
  46.3 0.2 fusion.35
  46.5 0.3 subtract_reduce_fusion.3
  47.0 0.7 %copy.19 = f32[2,2,5,16,256]{4,3,2,1,0:T(8,128)} copy(f32[2,2,5,16,256]{4,3,2,0,1:T(8,128)S(1)} %get-tuple-element.231) | data formatting | bytes 655360 | tf_op jit(solution)/shard_map/while | solution.py:166
  (56 shorter events, 1.8 us)
Async XLA Ops:
  0.0 6.2 %copy-start.1 = (f32[16,256]{1,0:T(8,128)S(1)}, f32[16,256]{1,0:T(8,128)}, u32[]{:S(2)}) copy-start(f32[16,256]{1,0:T(8,128)} %param.11) | copy-start | bytes 49156
  0.0 6.4 %copy-start.2 = (f32[2,2,3,16,256]{4,3,2,1,0:T(8,128)S(1)}, f32[2,2,3,16,256]{4,3,2,1,0:T(8,128)}, u32[]{:S(2)}) copy-start(f32[2,2,3,16,256]{4,3,2,1,0:T(8,128)} %param.10) | copy-start | bytes 589828
  1.1 15.2 %collective-permute-start.2 = (f32[21,1,256]{2,1,0:T(1,128)S(1)}, f32[21,1,256]{2,1,0:T(1,128)S(1)}, u32[]{:S(2)}, u32[]{:S(2)}) collective-permute-start(f32[21,1,256]{2,1,0:T(1,128)S(1)} %get-tuple-element.304), channel_id=1, source_target_pairs={{1,0},{2,1},{3,2},{0,3},{5,4},{6,5},{7,6},{4,7},{9,8},{10,9},{11,1... | collective-permute-start | bytes 64520 | tf_op jit(solution)/shard_map/ppermute | solution.py:19
  6.2 10.1 %collective-permute-start.1 = (f32[21,1,256]{2,1,0:T(1,128)S(1)}, f32[21,1,256]{2,1,0:T(1,128)S(1)}, u32[]{:S(2)}, u32[]{:S(2)}) collective-permute-start(f32[21,1,256]{2,1,0:T(1,128)S(1)} %get-tuple-element.303), channel_id=1, source_target_pairs={{0,1},{1,2},{2,3},{3,0},{4,5},{5,6},{6,7},{7,4},{8,9},{9,10},{10,1... | collective-permute-start | bytes 64520 | tf_op jit(solution)/shard_map/ppermute | solution.py:17
  15.0 0.7 %copy-start.3 = (s32[4]{0:T(128)S(1)}, s32[4]{0:T(128)}, u32[]{:S(2)}) copy-start(s32[4]{0:T(128)} %constant.163) | copy-start | bytes 52
  16.3 1.0 %copy-start = (f32[2,2,5,16,256]{4,3,2,1,0:T(8,128)S(1)}, f32[2,2,5,16,256]{4,3,2,1,0:T(8,128)}, u32[]{:S(2)}) copy-start(f32[2,2,5,16,256]{4,3,2,1,0:T(8,128)} %param.9) | copy-start | bytes 983044
  18.8 8.3 %collective-permute-start = (f32[2,2,5,18,256]{4,3,2,0,1:T(8,128)S(1)}, f32[2,2,5,18,256]{4,3,2,0,1:T(8,128)S(1)}, u32[]{:S(2)}, u32[]{:S(2)}) collective-permute-start(f32[2,2,5,18,256]{4,3,2,0,1:T(8,128)S(1)} %get-tuple-element.397), channel_id=1, source_target_pairs={{0,4},{4,8},{8,12},{12,0},{1,5},{5,9},{9,13},{13,1},{2,6},{6,10},{... | collective-permute-start | bytes 1105928 | tf_op jit(solution)/shard_map/while/body/eval_jaxpr/ppermute | solution.py:29
  28.2 8.3 %collective-permute-start = (f32[2,2,5,18,256]{4,3,2,0,1:T(8,128)S(1)}, f32[2,2,5,18,256]{4,3,2,0,1:T(8,128)S(1)}, u32[]{:S(2)}, u32[]{:S(2)}) collective-permute-start(f32[2,2,5,18,256]{4,3,2,0,1:T(8,128)S(1)} %get-tuple-element.397), channel_id=1, source_target_pairs={{0,4},{4,8},{8,12},{12,0},{1,5},{5,9},{9,13},{13,1},{2,6},{6,10},{... | collective-permute-start | bytes 1105928 | tf_op jit(solution)/shard_map/while/body/eval_jaxpr/ppermute | solution.py:29
  37.6 8.3 %collective-permute-start = (f32[2,2,5,18,256]{4,3,2,0,1:T(8,128)S(1)}, f32[2,2,5,18,256]{4,3,2,0,1:T(8,128)S(1)}, u32[]{:S(2)}, u32[]{:S(2)}) collective-permute-start(f32[2,2,5,18,256]{4,3,2,0,1:T(8,128)S(1)} %get-tuple-element.397), channel_id=1, source_target_pairs={{0,4},{4,8},{8,12},{12,0},{1,5},{5,9},{9,13},{13,1},{2,6},{6,10},{... | collective-permute-start | bytes 1105928 | tf_op jit(solution)/shard_map/while/body/eval_jaxpr/ppermute | solution.py:29
where the time goes:
time: 47.9 us; the launch traced here: 47.7 us
  waiting for transfers between devices  22.2 us (46%)
  blocking collectives  8.61 us (18%)
  local copies, waits for them, and re-layouts  6.52 us (14%)
  starting transfers between devices  5.65 us (12%)
  other arithmetic  4.13 us (9%)
    ppermute x3, waiting for transfers between devices, shifted(): return lax.ppermute(value, axis, pairs)  22.2 us
    all_gather x1, blocking collectives, shards(): whole_base = lax.all_gather(base_flow, 'harm', axis=0, tiled=True)  8.61 us
    ppermute x1, starting transfers between devices, extended(): lax.ppermute(head, axis, [((i + 1) % count, i) for i in range(count)])  5.13 us
    gather x4, local copies, waits for them, and re-layouts, block_terms(): chosen = blocks[index_table]  2.3 us
    unnamed x11, local copies, waits for them, and re-layouts  1.54 us
    reduce_sum x4, other arithmetic, block_terms(): jnp.sum(real_part, axis=1)  1.12 us
    slice x1, other arithmetic, extended(): lax.slice_in_dim(cells, cells.shape[dim] - width, cells.shape[dim], axis=...  1.1 us
    slice x8, local copies, waits for them, and re-layouts, split_rows(): grad_y = 0.5 * (jnp.roll(middle, -1, -1) - jnp.roll(middle, 1, -1))  1.09 us
  transfers between devices with their start and end apart: 5, of which 3 were waited for; matrix products, arithmetic and copies ran while one was open for 6% of the time, Pallas kernels for 0%

commit v1 on v0

--- a/solution.py
+++ b/solution.py
@@ -5,6 +5,18 @@
 from jax.sharding import PartitionSpec as P
 
 omega_base = 0.25
+
+
+def gather_by_bits(value, axis, dim):
+    ways, here = (lax.axis_size(axis), lax.axis_index(axis))
+    grown, reach = (value, 1)
+    while reach < ways:
+        theirs = lax.ppermute(grown, axis, [(d, d ^ reach) for d in range(ways)])
+        mine_first = jnp.concatenate([grown, theirs], axis=dim)
+        theirs_first = jnp.concatenate([theirs, grown], axis=dim)
+        grown = jnp.where(here & reach == 0, mine_first, theirs_first)
+        reach = 2 * reach
+    return grown
 
 
 def extended(cells, sides, width):
@@ -137,7 +149,7 @@
     frequency = (omega_base * signed.astype(jnp.float32)).reshape(local_count, 1, 1, 1)
     middle, grad_x, grad_y = split_rows(own_padded)
     summed = own_terms(middle, grad_x, grad_y, diffusion(own_padded, visc_padded), frequency)
-    whole_base = lax.all_gather(base_flow, "harm", axis=0, tiled=True)
+    whole_base = gather_by_bits(base_flow, "harm", 0)
 
     def base_pair(position, earlier):
         before = lax.dynamic_slice_in_dim(

time: 47.9 us -> 60.7 us (1.27)
  waiting for transfers between devices: 22.2 us -> 35.1 us
  blocking collectives: 8.61 us -> 0 us
  local copies, waits for them, and re-layouts: 6.52 us -> 12.2 us
  other arithmetic: 4.13 us -> 5.96 us
  starting transfers between devices: 5.65 us -> 6.78 us
    all_gather x1 -> x0, blocking collectives: 8.61 us -> none  [shards(): whole_base = lax.all_gather(base_flow, 'harm', axis=0, tiled=True)]
    ppermute x0 -> x2, waiting for transfers between devices: none -> 7.07 us  [gather_by_bits(): theirs = lax.ppermute(grown, axis, [(d, d ^ reach) for d in range(ways)])]
    ppermute x1, waiting for transfers between devices: 0.01 us -> 4.1 us  [extended(): lax.ppermute(tail, axis, [(i, (i + 1) % count) for i in range(count)])]
    while x3, local copies, waits for them, and re-layouts: 0.1 us -> 2.38 us
    ppermute x0 -> x2, starting transfers between devices: none -> 1.59 us  [gather_by_bits(): theirs = lax.ppermute(grown, axis, [(d, d ^ reach) for d in range(ways)])]
    unnamed x11 -> x23, local copies, waits for them, and re-layouts: 1.54 us -> 2.68 us
    reduce_sum x4, other arithmetic: 1.12 us -> 2.19 us  [block_terms(): jnp.sum(real_part, axis=1)]
    ppermute x3, waiting for transfers between devices: 22.2 us -> 23.2 us  [shifted(): return lax.ppermute(value, axis, pairs)]
  transfers between devices with their start and end apart: 5 -> 7, of which waited for: 3 -> 6; matrix products, arithmetic and copies ran while one was open for 6% -> 10% of each run, Pallas kernels for 0% -> 0%
where the time goes in v1:
time: 60.7 us; the launch traced here: 60.5 us
  waiting for transfers between devices  35.1 us (58%)
  local copies, waits for them, and re-layouts  12.2 us (20%)
  starting transfers between devices  6.78 us (11%)
  other arithmetic  5.96 us (10%)
    ppermute x3, waiting for transfers between devices, shifted(): return lax.ppermute(value, axis, pairs)  23.2 us
    ppermute x2, waiting for transfers between devices, gather_by_bits(): theirs = lax.ppermute(grown, axis, [(d, d ^ reach) for d in range(ways)])  7.07 us
    ppermute x1, starting transfers between devices, extended(): lax.ppermute(head, axis, [((i + 1) % count, i) for i in range(count)])  5.13 us
    ppermute x1, waiting for transfers between devices, extended(): lax.ppermute(tail, axis, [(i, (i + 1) % count) for i in range(count)])  4.1 us
    unnamed x23, local copies, waits for them, and re-layouts  2.68 us
    while x3, local copies, waits for them, and re-layouts  2.38 us
    gather x4, local copies, waits for them, and re-layouts, block_terms(): chosen = blocks[index_table]  2.3 us
    reduce_sum x4, other arithmetic, block_terms(): jnp.sum(real_part, axis=1)  2.19 us
  transfers between devices with their start and end apart: 7, of which 6 were waited for; matrix products, arithmetic and copies ran while one was open for 10% of the time, Pallas kernels for 0%

profile of v1, /device:TPU:0, one launch (start us, length us, event | category | flops | bytes accessed | tf_op | source)
XLA Modules:
  0.0 60.5 jit_solution(10231542549832963269)
XLA Ops:
  0.0 1.1 %pad_maximum_fusion.8 = (f32[21,1,256]{2,1,0:T(1,128)S(1)}, f32[21,1,256]{2,1,0:T(1,128)S(1)}) fusion(f32[1,16,256]{2,1,0:T(8,128)} %bitcast.94, f32[20,16,256]{2,1,0:T(8,128)} %bitcast.90), kind=kLoop, calls=%fused_computation.59 | loop fusion | flops 10752 | bytes 387072 | tf_op jit(solution)/shard_map/slice | solution.py:26
  1.1 5.1 %collective-permute-start.2 = (f32[21,1,256]{2,1,0:T(1,128)S(1)}, f32[21,1,256]{2,1,0:T(1,128)S(1)}, u32[]{:S(2)}, u32[]{:S(2)}) collective-permute-start(f32[21,1,256]{2,1,0:T(1,128)S(1)} %get-tuple-element.304), channel_id=1, source_target_pairs={{1,0},{2,1},{3,2},{0,3},{5,4},{6,5},{7,6},{4,7},{9,8},{10,9},{11,1... | collective-permute-start | bytes 64520 | tf_op jit(solution)/shard_map/ppermute | solution.py:31
  6.4 0.7 %copy-done.9 = s32[4]{0:T(128)S(1)} copy-done((s32[4]{0:T(128)S(1)}, s32[4]{0:T(128)}, u32[]{:S(2)}) %copy-start.9) | copy-done | bytes 40
  7.1 0.7 %collective-permute-done.2 = f32[21,1,256]{2,1,0:T(1,128)S(1)} collective-permute-done((f32[21,1,256]{2,1,0:T(1,128)S(1)}, f32[21,1,256]{2,1,0:T(1,128)S(1)}, u32[]{:S(2)}, u32[]{:S(2)}) %collective-permute-start.2) | collective-permute-done | bytes 21536 | tf_op jit(solution)/shard_map/ppermute | solution.py:31
  7.7 4.1 %collective-permute-done.1 = f32[21,1,256]{2,1,0:T(1,128)S(1)} collective-permute-done((f32[21,1,256]{2,1,0:T(1,128)S(1)}, f32[21,1,256]{2,1,0:T(1,128)S(1)}, u32[]{:S(2)}, u32[]{:S(2)}) %collective-permute-start.1) | collective-permute-done | bytes 21536 | tf_op jit(solution)/shard_map/ppermute | solution.py:29
  12.2 0.2 subtract_multiply_fusion
  12.4 0.7 %slice_bitcast_fusion.13 = (f32[2,5,16,256]{3,2,1,0:T(8,128)}, f32[2,5,16,256]{3,2,1,0:T(8,128)}) fusion(f32[2,2,5,16,256]{4,3,2,0,1:T(8,128)S(1)} %get-tuple-element.315), kind=kLoop, calls=%fused_computation.41 | loop fusion | bytes 655360 | tf_op jit(solution)/shard_map/mul | solution.py:85
  13.2 0.8 %slice_bitcast_fusion.15 = (f32[2,5,16,256]{3,2,1,0:T(8,128)}, f32[2,5,16,256]{3,2,1,0:T(8,128)}) fusion(f32[2,2,5,16,256]{4,3,2,0,1:T(8,128)S(1)} %get-tuple-element.316), kind=kLoop, calls=%fused_computation.43 | loop fusion | bytes 655360 | tf_op jit(solution)/shard_map/mul | solution.py:83
  14.0 0.8 %copy.9 = f32[2,2,5,18,256]{4,3,2,0,1:T(8,128)} copy(f32[2,2,5,18,256]{4,3,2,1,0:T(8,128)S(1)} %bitcast.85) | data formatting | bytes 737280 | tf_op jit(solution)/shard_map/reshape | solution.py:144
  14.9 0.9 %copy-done.8 = f32[2,2,3,16,256]{4,3,2,1,0:T(8,128)S(1)} copy-done((f32[2,2,3,16,256]{4,3,2,1,0:T(8,128)S(1)}, f32[2,2,3,16,256]{4,3,2,1,0:T(8,128)}, u32[]{:S(2)}) %copy-start.8) | copy-done | bytes 196632
  15.8 1.6 %collective-permute-start.4 = (f32[4,2,3,16,256]{4,3,2,1,0:T(8,128)S(1)}, f32[4,2,3,16,256]{4,3,2,1,0:T(8,128)S(1)}, u32[]{:S(2)}, u32[]{:S(2)}) collective-permute-start(f32[4,2,3,16,256]{4,3,2,1,0:T(8,128)S(1)} %maximum_select_fusion.1), channel_id=1, source_target_pairs={{0,8},{4,12},{8,0},{12,4},{1,9},{5,13},{9,1},{13,5},{2,10},{6,14},... | collective-permute-start | bytes 1179656 | tf_op jit(solution)/shard_map/ppermute | solution.py:14
  17.5 0.8 %slice_bitcast_fusion.16 = (f32[2,5,16,256]{3,2,1,0:T(8,128)}, f32[2,5,16,256]{3,2,1,0:T(8,128)}, f32[2,1,5,16,256]{4,3,2,0,1:T(8,128)S(1)}, f32[2,1,5,16,256]{4,3,2,0,1:T(8,128)S(1)}) fusion(f32[2]{0:T(128)S(1)} %get-tuple-element.317, f32[2]{0:T(128)S(1)} %get-tuple-element.318, f32[2,2,5,18,256]{4,3,2,1,0:T(8,128)S(1)} %bitcast.86), kind=kLoop, calls=%fused_computation.44 | loop fusion | flops 81920 | bytes 984064 | tf_op jit(solution)/shard_map/mul | solution.py:87
  18.2 7.1 %collective-permute-done.4 = f32[4,2,3,16,256]{4,3,2,1,0:T(8,128)S(1)} collective-permute-done((f32[4,2,3,16,256]{4,3,2,1,0:T(8,128)S(1)}, f32[4,2,3,16,256]{4,3,2,1,0:T(8,128)S(1)}, u32[]{:S(2)}, u32[]{:S(2)}) %collective-permute-start.4) | collective-permute-done | bytes 393248 | tf_op jit(solution)/shard_map/ppermute | solution.py:14
  25.5 0.6 gather_fusion.1
  26.1 0.8 %copy-done.2 = f32[2,5,16,256]{3,2,1,0:T(8,128)S(1)} copy-done((f32[2,5,16,256]{3,2,1,0:T(8,128)S(1)}, f32[2,5,16,256]{3,2,1,0:T(8,128)}, u32[]{:S(2)}) %copy-start.2) | copy-done | bytes 163864
  27.2 1.3 %subtract_reduce_fusion.1 = (f32[2,5,16,256]{3,2,1,0:T(8,128)S(1)}, f32[2,5,16,256]{3,2,1,0:T(8,128)S(1)}) fusion(f32[2,5,16,256]{3,2,1,0:T(8,128)} %get-tuple-element.288, f32[2,2,16,256]{3,2,1,0:T(8,128)S(1)} %get-tuple-element.300, f32[2,5,16,256]{3,2,1,0:T(8,128)} %get-tuple-element.287, f32[2,2,16,256]{3,2,1,0:T(8,128)S(1)} %get-tuple-element.296, ...), kind=kLoop, calls=%fused_computation.37 | loop fusion | flops 1884160 | bytes 1703936 | tf_op jit(solution)/shard_map/reduce_sum | solution.py:132
  28.6 0.3 fusion.3
  28.9 30.9 %while.21 = (s32[]{:T(128)}, f32[2,2,5,16,256]{4,3,2,0,1:T(8,128)S(1)}, f32[2,2,5,18,256]{4,3,2,0,1:T(8,128)}, f32[8,2,3,16,256]{4,3,2,1,0:T(8,128)S(1)}, s32[]{...) while((s32[]{:T(128)}, ...), condition=%wide.region_5.6_spmd.clone, body=%wide.region_2.5_spmd.sunk.clone.sunk | while | flops 2638870 | bytes 13291922 | solution.py:178
  29.1 0.6 gather_fusion
  29.7 7.7 %collective-permute-done = f32[2,2,5,18,256]{4,3,2,0,1:T(8,128)S(1)} collective-permute-done((f32[2,2,5,18,256]{4,3,2,0,1:T(8,128)}, f32[2,2,5,18,256]{4,3,2,0,1:T(8,128)S(1)}, u32[]{:S(2)}, u32[]{:S(2)}) %collective-permute-start) | collective-permute-done | bytes 368672 | tf_op jit(solution)/shard_map/while/body/eval_jaxpr/ppermute | solution.py:41
  37.8 0.2 fusion.35
  38.0 0.3 subtract_reduce_fusion.3
  38.4 0.8 %copy.42 = f32[2,2,5,18,256]{4,3,2,0,1:T(8,128)} copy(f32[2,2,5,18,256]{4,3,2,0,1:T(8,128)S(1)} %collective-permute-done) | data formatting | bytes 737280 | tf_op jit(solution)/shard_map/while
  39.3 0.6 gather_fusion
  39.9 7.8 %collective-permute-done = f32[2,2,5,18,256]{4,3,2,0,1:T(8,128)S(1)} collective-permute-done((f32[2,2,5,18,256]{4,3,2,0,1:T(8,128)}, f32[2,2,5,18,256]{4,3,2,0,1:T(8,128)S(1)}, u32[]{:S(2)}, u32[]{:S(2)}) %collective-permute-start) | collective-permute-done | bytes 368672 | tf_op jit(solution)/shard_map/while/body/eval_jaxpr/ppermute | solution.py:41
  48.3 0.3 subtract_reduce_fusion.3
  48.7 0.8 %copy.42 = f32[2,2,5,18,256]{4,3,2,0,1:T(8,128)} copy(f32[2,2,5,18,256]{4,3,2,0,1:T(8,128)S(1)} %collective-permute-done) | data formatting | bytes 737280 | tf_op jit(solution)/shard_map/while
  49.6 0.6 gather_fusion
  50.2 7.8 %collective-permute-done = f32[2,2,5,18,256]{4,3,2,0,1:T(8,128)S(1)} collective-permute-done((f32[2,2,5,18,256]{4,3,2,0,1:T(8,128)}, f32[2,2,5,18,256]{4,3,2,0,1:T(8,128)S(1)}, u32[]{:S(2)}, u32[]{:S(2)}) %collective-permute-start) | collective-permute-done | bytes 368672 | tf_op jit(solution)/shard_map/while/body/eval_jaxpr/ppermute | solution.py:41
  58.6 0.3 subtract_reduce_fusion.3
  59.0 0.8 %copy.42 = f32[2,2,5,18,256]{4,3,2,0,1:T(8,128)} copy(f32[2,2,5,18,256]{4,3,2,0,1:T(8,128)S(1)} %collective-permute-done) | data formatting | bytes 737280 | tf_op jit(solution)/shard_map/while
  59.8 0.7 %copy.19 = f32[2,2,5,16,256]{4,3,2,1,0:T(8,128)} copy(f32[2,2,5,16,256]{4,3,2,0,1:T(8,128)S(1)} %get-tuple-element.231) | data formatting | bytes 655360 | tf_op jit(solution)/shard_map/while | solution.py:178
  (73 shorter events, 3.3 us)
Async XLA Ops:
  0.0 11.9 %copy-start = (f32[2,2,5,16,256]{4,3,2,1,0:T(8,128)S(1)}, f32[2,2,5,16,256]{4,3,2,1,0:T(8,128)}, u32[]{:S(2)}) copy-start(f32[2,2,5,16,256]{4,3,2,1,0:T(8,128)} %param.9) | copy-start | bytes 983044
  0.0 6.3 %copy-start.1 = (f32[16,256]{1,0:T(8,128)S(1)}, f32[16,256]{1,0:T(8,128)}, u32[]{:S(2)}) copy-start(f32[16,256]{1,0:T(8,128)} %param.11) | copy-start | bytes 49156
  1.1 6.6 %collective-permute-start.2 = (f32[21,1,256]{2,1,0:T(1,128)S(1)}, f32[21,1,256]{2,1,0:T(1,128)S(1)}, u32[]{:S(2)}, u32[]{:S(2)}) collective-permute-start(f32[21,1,256]{2,1,0:T(1,128)S(1)} %get-tuple-element.304), channel_id=1, source_target_pairs={{1,0},{2,1},{3,2},{0,3},{5,4},{6,5},{7,6},{4,7},{9,8},{10,9},{11,1... | collective-permute-start | bytes 64520 | tf_op jit(solution)/shard_map/ppermute | solution.py:31
  6.3 5.6 %collective-permute-start.1 = (f32[21,1,256]{2,1,0:T(1,128)S(1)}, f32[21,1,256]{2,1,0:T(1,128)S(1)}, u32[]{:S(2)}, u32[]{:S(2)}) collective-permute-start(f32[21,1,256]{2,1,0:T(1,128)S(1)} %get-tuple-element.303), channel_id=1, source_target_pairs={{0,1},{1,2},{2,3},{3,0},{4,5},{5,6},{6,7},{7,4},{8,9},{9,10},{10,1... | collective-permute-start | bytes 64520 | tf_op jit(solution)/shard_map/ppermute | solution.py:29
  6.3 8.6 %collective-permute-start.3 = (f32[2,2,3,16,256]{4,3,2,1,0:T(8,128)}, f32[2,2,3,16,256]{4,3,2,1,0:T(8,128)S(1)}, u32[]{:S(2)}, u32[]{:S(2)}) collective-permute-start(f32[2,2,3,16,256]{4,3,2,1,0:T(8,128)} %param.10), channel_id=1, source_target_pairs={{0,4},{4,0},{8,12},{12,8},{1,5},{5,1},{9,13},{13,9},{2,6},{6,2},{1... | collective-permute-start | bytes 589832 | tf_op jit(solution)/shard_map/ppermute | solution.py:14
  6.4 0.7 %copy-start.9 = (s32[4]{0:T(128)S(1)}, s32[4]{0:T(128)}, u32[]{:S(2)}) copy-start(s32[4]{0:T(128)} %constant.164) | copy-start | bytes 52
  14.8 1.0 %copy-start.8 = (f32[2,2,3,16,256]{4,3,2,1,0:T(8,128)S(1)}, f32[2,2,3,16,256]{4,3,2,1,0:T(8,128)}, u32[]{:S(2)}) copy-start(f32[2,2,3,16,256]{4,3,2,1,0:T(8,128)} %param.10) | copy-start | bytes 589828
  14.9 1.0 %copy-start.6 = (f32[2,2,5,16,256]{4,3,2,0,1:T(8,128)}, f32[2,2,5,16,256]{4,3,2,0,1:T(8,128)S(1)}, u32[]{:S(2)}) copy-start(f32[2,2,5,16,256]{4,3,2,0,1:T(8,128)S(1)} %fusion.5) | copy-start | bytes 983044
  15.8 9.5 %collective-permute-start.4 = (f32[4,2,3,16,256]{4,3,2,1,0:T(8,128)S(1)}, f32[4,2,3,16,256]{4,3,2,1,0:T(8,128)S(1)}, u32[]{:S(2)}, u32[]{:S(2)}) collective-permute-start(f32[4,2,3,16,256]{4,3,2,1,0:T(8,128)S(1)} %maximum_select_fusion.1), channel_id=1, source_target_pairs={{0,8},{4,12},{8,0},{12,4},{1,9},{5,13},{9,1},{13,5},{2,10},{6,14},... | collective-permute-start | bytes 1179656 | tf_op jit(solution)/shard_map/ppermute | solution.py:14
  26.0 0.9 %copy-start.2 = (f32[2,5,16,256]{3,2,1,0:T(8,128)S(1)}, f32[2,5,16,256]{3,2,1,0:T(8,128)}, u32[]{:S(2)}) copy-start(f32[2,5,16,256]{3,2,1,0:T(8,128)} %get-tuple-element.307) | copy-start | bytes 491524
  26.1 1.0 %copy-start.3 = (f32[2,5,16,256]{3,2,1,0:T(8,128)S(1)}, f32[2,5,16,256]{3,2,1,0:T(8,128)}, u32[]{:S(2)}) copy-start(f32[2,5,16,256]{3,2,1,0:T(8,128)} %get-tuple-element.308) | copy-start | bytes 491524
  26.1 1.1 %copy-start.4 = (f32[2,5,16,256]{3,2,1,0:T(8,128)S(1)}, f32[2,5,16,256]{3,2,1,0:T(8,128)}, u32[]{:S(2)}) copy-start(f32[2,5,16,256]{3,2,1,0:T(8,128)} %get-tuple-element.305) | copy-start | bytes 491524
  26.1 1.1 %copy-start.5 = (f32[2,5,16,256]{3,2,1,0:T(8,128)S(1)}, f32[2,5,16,256]{3,2,1,0:T(8,128)}, u32[]{:S(2)}) copy-start(f32[2,5,16,256]{3,2,1,0:T(8,128)} %get-tuple-element.306) | copy-start | bytes 491524
  27.2 1.4 %copy-start.7 = (f32[2,2,5,16,256]{4,3,2,0,1:T(8,128)S(1)}, f32[2,2,5,16,256]{4,3,2,0,1:T(8,128)}, u32[]{:S(2)}) copy-start(f32[2,2,5,16,256]{4,3,2,0,1:T(8,128)} %copy-done.6) | copy-start | bytes 983044
  28.9 8.5 %collective-permute-start = (f32[2,2,5,18,256]{4,3,2,0,1:T(8,128)}, f32[2,2,5,18,256]{4,3,2,0,1:T(8,128)S(1)}, u32[]{:S(2)}, u32[]{:S(2)}) collective-permute-start(f32[2,2,5,18,256]{4,3,2,0,1:T(8,128)} %get-tuple-element.397), channel_id=1, source_target_pairs={{0,4},{4,8},{8,12},{12,0},{1,5},{5,9},{9,13},{13,1},{2,6},{6,10},{... | collective-permute-start | bytes 1105928 | tf_op jit(solution)/shard_map/while/body/eval_jaxpr/ppermute | solution.py:41
  39.2 8.5 %collective-permute-start = (f32[2,2,5,18,256]{4,3,2,0,1:T(8,128)}, f32[2,2,5,18,256]{4,3,2,0,1:T(8,128)S(1)}, u32[]{:S(2)}, u32[]{:S(2)}) collective-permute-start(f32[2,2,5,18,256]{4,3,2,0,1:T(8,128)} %get-tuple-element.397), channel_id=1, source_target_pairs={{0,4},{4,8},{8,12},{12,0},{1,5},{5,9},{9,13},{13,1},{2,6},{6,10},{... | collective-permute-start | bytes 1105928 | tf_op jit(solution)/shard_map/while/body/eval_jaxpr/ppermute | solution.py:41
  49.5 8.5 %collective-permute-start = (f32[2,2,5,18,256]{4,3,2,0,1:T(8,128)}, f32[2,2,5,18,256]{4,3,2,0,1:T(8,128)S(1)}, u32[]{:S(2)}, u32[]{:S(2)}) collective-permute-start(f32[2,2,5,18,256]{4,3,2,0,1:T(8,128)} %get-tuple-element.397), channel_id=1, source_target_pairs={{0,4},{4,8},{8,12},{12,0},{1,5},{5,9},{9,13},{13,1},{2,6},{6,10},{... | collective-permute-start | bytes 1105928 | tf_op jit(solution)/shard_map/while/body/eval_jaxpr/ppermute | solution.py:41
